TPU v7x, 256 devices: a whole 4x4x8 slice. The times are simulated.
256 devices in a mesh: seq: 32 (over z, y_lo, core), tp: 8 (over x, y_hi).
Axes of the slice: x: 4, y: 4 (y_hi: 2, y_lo: 2; y = y_hi * 2 + y_lo), z: 8, core: 2. Of those that a mesh axis runs over, the one named last changes fastest.
Arguments:
- grad_out: bfloat16 [8192, 14336], P('seq', 'tp'), may hold values from -6 to 6
- weight: bfloat16 [4096, 14336], P('seq', 'tp'), may hold values from -0.046875 to 0.046875
- saved: bfloat16 [8192, 512], P('seq'), may hold values from -0.125 to 0.125
- first_moment: float32 [512, 14336], P('seq', 'tp'), may hold values from -6 to 6
- second_moment: float32 [512, 14336], P('seq', 'tp'), may hold values from 0.05 to 2
- basis: bfloat16 [4096, 512], P('seq'), may hold values from -0.0625 to 0.0625
- new_basis: bfloat16 [4096, 512], P('seq'), may hold values from -0.09375 to 0.09375
Outputs:
- grad_input: float32 [8192, 4096], P('seq', 'tp')
- first_new: float32 [512, 14336], P('seq', 'tp')
- second_new: float32 [512, 14336], P('seq', 'tp')
- update: float32 [512, 14336], P('seq', 'tp')
All inputs are finite; a program needn't handle non-finite values.
Results may differ from a plain program's by a relative error of at most 0.0003.
Values may be sent and summed in bfloat16 or wider, within the bound.
A program may use at most 128 MiB of HBM per device.

v0:
```python
import jax
import jax.numpy as jnp
from jax import lax
from jax.sharding import PartitionSpec as P


def contract_rows(left, right):
    return lax.dot_general(
        left, right, (((0,), (0,)), ((), ())), preferred_element_type=jnp.float32
    )


def exact_dot(left, right):
    return jnp.dot(left, right, precision=lax.Precision.HIGHEST, preferred_element_type=jnp.float32)


def per_device(grad_out, weight, saved, first_moment, second_moment, basis, new_basis):
    rank_rows = first_moment.shape[0]
    row_start = lax.axis_index("seq") * rank_rows
    partial_input = lax.dot_general(
        grad_out,
        lax.all_gather(weight, "seq", axis=0, tiled=True),
        (((1,), (1,)), ((), ())),
        preferred_element_type=jnp.float32,
    )
    grad_input = lax.psum_scatter(partial_input, "tp", scatter_dimension=1, tiled=True)
    local_intersection = contract_rows(new_basis, basis)
    intersection = lax.psum(local_intersection, "seq")
    gradient = lax.psum_scatter(
        contract_rows(saved, grad_out), "seq", scatter_dimension=0, tiled=True
    )
    full_first, full_second = (
        lax.all_gather(first_moment, "seq", axis=0, tiled=True),
        lax.all_gather(second_moment, "seq", axis=0, tiled=True),
    )
    own_rows = lax.dynamic_slice_in_dim(intersection, row_start, rank_rows, 0)
    first_rot = exact_dot(own_rows, full_first)
    second_rot = exact_dot(own_rows * own_rows, full_second)
    first_new = 0.9 * first_rot + 0.1 * gradient
    second_new = 0.95 * second_rot + 0.05 * gradient * gradient
    update = first_new / (jnp.sqrt(second_new) + 1e-08)
    return (grad_input, first_new, second_new, update)


def solution(mesh):
    return jax.shard_map(
        per_device,
        mesh=mesh,
        in_specs=(
            P("seq", "tp"),
            P("seq", "tp"),
            P("seq", None),
            P("seq", "tp"),
            P("seq", "tp"),
            P("seq", None),
            P("seq", None),
        ),
        out_specs=(P("seq", "tp"), P("seq", "tp"), P("seq", "tp"), P("seq", "tp")),
        check_vma=False,
    )
```

profile of v0, /device:TPU:2, one launch (start us, length us, event | category | flops | bytes accessed | tf_op | source)
XLA Modules:
  0.0 695.8 jit_solution(15503047025166529226)
XLA Ops:
  7.2 0.0 copy-start
  7.2 0.0 all-gather.4.cloned.1.call-start
  7.2 0.7 all-gather.4.cloned.1.call-update
  7.9 0.0 all-reduce.2.cloned.1.call-start
  8.0 2.2 fusion.8
  10.2 0.0 all-reduce.2.cloned.1.call-update
  10.2 0.0 all-gather.8.cloned.1.call-start
  10.3 0.7 all-gather.8.cloned.1.call-update
  11.0 0.0 reduce-scatter.5.cloned.1.call-start
  11.0 0.0 copy-done
  11.0 3.5 fusion.9
  14.5 0.0 reduce-scatter.5.cloned.1.call-update
  14.5 0.0 all-gather.6.cloned.1.call-start
  14.6 0.5 all-gather.6.cloned.1.call-update
  15.1 0.0 reduce-scatter.3.cloned.1.call-start
  15.2 86.8 %all-gather.4.cloned.1.call-done = bf16[4096,1792]{1,0:T(8,128)(2,1)} async-done(((bf16[128,1792]{1,0:T(8,128)(2,1)}), bf16[4096,1792]{1,0:T(8,128)(2,1)}) %all-gather.4.cloned.1.call-update) | async-done | bytes 14680080 | tf_op jit(solution)/shard_map/all_gather | solution.py:22
  102.0 16.0 %fusion.7 = f32[256,4096]{1,0:T(8,128)} fusion(bf16[256,1792]{1,0:T(8,128)(2,1)S(1)} %copy-done, bf16[4096,1792]{1,0:T(8,128)(2,1)} %all-gather.4.cloned.1.call-done), kind=kOutput, calls=%fused_computation.11 | convolution fusion | flops 3758096384 | bytes 19791872 | tf_op jit(solution)/shard_map/dot_general | solution.py:20
  118.0 0.0 reduce-scatter.3.cloned.1.call-update
  118.0 216.1 %all-reduce.2.cloned.1.call-done = f32[512,512]{1,0:T(8,128)} async-done(((f32[512,512]{1,0:T(8,128)}), f32[512,512]{1,0:T(8,128)}) %all-reduce.2.cloned.1.call-update) | async-done | bytes 1048592 | tf_op jit(solution)/shard_map/psum | solution.py:28
  334.1 68.7 %all-gather.8.cloned.1.call-done = f32[512,1792]{1,0:T(8,128)} async-done(((f32[16,1792]{1,0:T(8,128)}), f32[512,1792]{1,0:T(8,128)}) %all-gather.8.cloned.1.call-update) | async-done | bytes 3670032 | tf_op jit(solution)/shard_map/all_gather | solution.py:34
  402.7 125.6 %reduce-scatter.5.cloned.1.call-done = f32[16,1792]{1,0:T(8,128)} async-done(((f32[512,1792]{1,0:T(8,128)}), f32[16,1792]{1,0:T(8,128)}) %reduce-scatter.5.cloned.1.call-update) | async-done | bytes 114704 | tf_op jit(solution)/shard_map/reduce_scatter | solution.py:29
  528.3 0.0 copy-start.1
  528.3 3.8 fusion
  532.2 0.0 copy-start.2
  532.2 62.1 %all-gather.6.cloned.1.call-done = f32[512,1792]{1,0:T(8,128)} async-done(((f32[16,1792]{1,0:T(8,128)}), f32[512,1792]{1,0:T(8,128)}) %all-gather.6.cloned.1.call-update) | async-done | bytes 3670032 | tf_op jit(solution)/shard_map/all_gather | solution.py:33
  594.3 0.0 copy-done.1
  594.3 4.5 add_divide_fusion
  598.9 90.0 %reduce-scatter.3.cloned.1.call-done = f32[256,512]{1,0:T(8,128)} async-done(((f32[256,4096]{1,0:T(8,128)}), f32[256,512]{1,0:T(8,128)}) %reduce-scatter.3.cloned.1.call-update) | async-done | bytes 524304 | tf_op jit(solution)/shard_map/reduce_scatter | solution.py:26
  688.9 0.0 copy-done.2
Async XLA Ops:
  7.2 3.8 copy-start
  7.2 94.8 %all-gather.4.cloned.1.call-start = ((), (), s32[]{:S(2)}) async-start(), calls=%async_computation.2 | async-start | bytes 15138816 | tf_op jit(solution)/shard_map/all_gather | solution.py:22
  7.9 326.1 %all-reduce.2.cloned.1.call-start = ((), (), s32[]{:S(2)}) async-start(), calls=%async_computation.4 | async-start | bytes 2097152 | tf_op jit(solution)/shard_map/psum | solution.py:28
  10.2 392.5 %all-gather.8.cloned.1.call-start = ((), (), s32[]{:S(2)}) async-start(), calls=%async_computation.7 | async-start | bytes 3784704 | tf_op jit(solution)/shard_map/all_gather | solution.py:34
  11.0 517.4 %reduce-scatter.5.cloned.1.call-start = ((), (), s32[]{:S(2)}) async-start(), calls=%async_computation.6 | async-start | bytes 3784704 | tf_op jit(solution)/shard_map/reduce_scatter | solution.py:29
  14.5 579.8 %all-gather.6.cloned.1.call-start = ((), (), s32[]{:S(2)}) async-start(), calls=%async_computation.5 | async-start | bytes 3784704 | tf_op jit(solution)/shard_map/all_gather | solution.py:33
  15.1 673.8 %reduce-scatter.3.cloned.1.call-start = ((), (), s32[]{:S(2)}) async-start(), calls=%async_computation.3 | async-start | bytes 4718592 | tf_op jit(solution)/shard_map/reduce_scatter | solution.py:26
  528.3 66.0 %copy-start.1 = (f32[16,1792]{1,0:T(8,128)S(1)}, f32[16,1792]{1,0:T(8,128)}, u32[]{:S(2)}) copy-start(f32[16,1792]{1,0:T(8,128)} %reduce-scatter.5.cloned.1.call-done) | copy-start | bytes 344068
  532.2 156.7 %copy-start.2 = (f32[16,1792]{1,0:T(8,128)}, f32[16,1792]{1,0:T(8,128)S(1)}, u32[]{:S(2)}) copy-start(f32[16,1792]{1,0:T(8,128)S(1)} %fusion) | copy-start | bytes 344068
Sparse Core Ops, SparseCore 0:
  9.8 92.0 all-gather.3
  104.6 229.4 all-reduce.1
  335.9 66.7 all-gather.7
  405.1 123.1 reduce-scatter.4
  530.0 64.2 all-gather.5
  598.9 89.9 reduce-scatter.2
where the time goes:
time: 696 us
  waiting for transfers between devices  651 us (94%)
  matrix products  30.1 us (4%)
  between operations  14.1 us (2%)
    psum x1, waiting for transfers between devices, per_device(): intersection = lax.psum(local_intersection, 'seq')  216 us
    reduce_scatter x1, waiting for transfers between devices, per_device(): lax.psum_scatter(contract_rows(saved, grad_out), 'seq', scatter_dimension...  126 us
    reduce_scatter x1, waiting for transfers between devices, per_device(): lax.psum_scatter(partial_input, 'tp', scatter_dimension=1, tiled=True)  90 us
    all_gather x1, waiting for transfers between devices, per_device(): lax.all_gather(weight, 'seq', axis=0, tiled=True)  86.8 us
    all_gather x1, waiting for transfers between devices, per_device(): lax.all_gather(second_moment, 'seq', axis=0, tiled=True)  68.7 us
    all_gather x1, waiting for transfers between devices, per_device(): lax.all_gather(first_moment, 'seq', axis=0, tiled=True)  62.1 us
    dot_general x1, matrix products, per_device(): lax.dot_general(grad_out, lax.all_gather(weight, 'seq', axis=0, tiled=Tru...  16 us
  transfers between devices with their start and end apart: 6, of which 6 were waited for; matrix products, arithmetic and copies ran while one was open for 4% of the time, Pallas kernels for 0%

commit v1 on v0

--- a/solution.py
+++ b/solution.py
@@ -30,7 +30,9 @@
         contract_rows(saved, grad_out), "seq", scatter_dimension=0, tiled=True
     )
     full_first, full_second = (
-        lax.all_gather(first_moment, "seq", axis=0, tiled=True),
+        jnp.concatenate(
+            lax.all_to_all(jnp.stack([first_moment] * lax.axis_size("seq")), "seq", 0, 0), axis=0
+        ),
         lax.all_gather(second_moment, "seq", axis=0, tiled=True),
     )
     own_rows = lax.dynamic_slice_in_dim(intersection, row_start, rank_rows, 0)

time: 696 us -> 649 us (0.932)
  waiting for transfers between devices: 651 us -> 594 us
  starting transfers between devices: 0.24 us -> 7.65 us
    all_gather x1 -> x0, waiting for transfers between devices: 62.1 us -> none  [per_device(): lax.all_gather(first_moment, 'seq', axis=0, tiled=True)]
    psum x1, waiting for transfers between devices: 216 us -> 226 us  [per_device(): intersection = lax.psum(local_intersection, 'seq')]
    all_to_all x0 -> x1, starting transfers between devices: none -> 7.46 us  [per_device(): lax.all_to_all(jnp.stack([first_moment] * lax.axis_size('seq')), 'seq', 0...]
  transfers between devices with their start and end apart: 6 -> 6, of which waited for: 6 -> 5; matrix products, arithmetic and copies ran while one was open for 4% -> 5% of each run, Pallas kernels for 0% -> 0%
where the time goes in v1:
time: 649 us; the launch traced here: 648 us
  waiting for transfers between devices  594 us (92%)
  matrix products  30.2 us (5%)
  between operations  13.8 us (2%)
  starting transfers between devices  7.65 us (1%)
    psum x1, waiting for transfers between devices, per_device(): intersection = lax.psum(local_intersection, 'seq')  226 us
    reduce_scatter x1, waiting for transfers between devices, per_device(): lax.psum_scatter(contract_rows(saved, grad_out), 'seq', scatter_dimension...  126 us
    all_gather x1, waiting for transfers between devices, per_device(): lax.all_gather(weight, 'seq', axis=0, tiled=True)  87.3 us
    reduce_scatter x1, waiting for transfers between devices, per_device(): lax.psum_scatter(partial_input, 'tp', scatter_dimension=1, tiled=True)  84.7 us
    all_gather x1, waiting for transfers between devices, per_device(): lax.all_gather(second_moment, 'seq', axis=0, tiled=True)  68.7 us
    dot_general x1, matrix products, per_device(): lax.dot_general(grad_out, lax.all_gather(weight, 'seq', axis=0, tiled=Tru...  16 us
  transfers between devices with their start and end apart: 6, of which 5 were waited for; matrix products, arithmetic and copies ran while one was open for 5% of the time, Pallas kernels for 0%

profile of v1, /device:TPU:2, one launch (start us, length us, event | category | flops | bytes accessed | tf_op | source)
XLA Modules:
  0.0 648.3 jit_solution(3584036406594591965)
XLA Ops:
  7.2 0.0 copy-start
  7.2 0.0 all-gather.3.cloned.1.call-start
  7.2 0.7 all-gather.3.cloned.1.call-update
  7.9 0.0 all-reduce.2.cloned.1.call-start
  8.0 2.3 fusion.8
  10.2 0.0 all-reduce.2.cloned.1.call-update
  10.2 0.0 all-gather.5.cloned.1.call-start
  10.3 0.7 all-gather.5.cloned.1.call-update
  11.0 0.0 reduce-scatter.5.cloned.1.call-start
  11.0 0.0 copy-done
  11.0 3.5 fusion.9
  14.5 0.0 reduce-scatter.5.cloned.1.call-update
  14.6 0.0 reduce-scatter.3.cloned.1.call-start
  14.6 87.3 %all-gather.3.cloned.1.call-done = bf16[4096,1792]{1,0:T(8,128)(2,1)} async-done(((bf16[128,1792]{1,0:T(8,128)(2,1)}), bf16[4096,1792]{1,0:T(8,128)(2,1)}) %all-gather.3.cloned.1.call-update) | async-done | bytes 14680080 | tf_op jit(solution)/shard_map/all_gather | solution.py:22
  102.0 16.0 %fusion.7 = f32[256,4096]{1,0:T(8,128)} fusion(bf16[256,1792]{1,0:T(8,128)(2,1)S(1)} %copy-done, bf16[4096,1792]{1,0:T(8,128)(2,1)} %all-gather.3.cloned.1.call-done), kind=kOutput, calls=%fused_computation.11 | convolution fusion | flops 3758096384 | bytes 19791872 | tf_op jit(solution)/shard_map/dot_general | solution.py:20
  118.0 0.0 copy-start.3
  118.0 0.0 reduce-scatter.3.cloned.1.call-update
  118.0 0.9 copy-done.3
  118.9 2.3 stack.2
  121.1 7.5 %all-to-all-start = ((f32[32,16,1792]{2,1,0:T(8,128)}), f32[32,16,1792]{2,1,0:T(8,128)}, u32[]{:S(2)}, u32[]{:S(2)}) async-start(f32[32,16,1792]{2,1,0:T(8,128)} %stack.2), calls=%async_computation.1 | async-start | bytes 7340032 | tf_op jit(solution)/shard_map/all_to_all | solution.py:34
  128.6 225.8 %all-reduce.2.cloned.1.call-done = f32[512,512]{1,0:T(8,128)} async-done(((f32[512,512]{1,0:T(8,128)}), f32[512,512]{1,0:T(8,128)}) %all-reduce.2.cloned.1.call-update) | async-done | bytes 1048592 | tf_op jit(solution)/shard_map/psum | solution.py:28
  354.4 68.7 %all-gather.5.cloned.1.call-done = f32[512,1792]{1,0:T(8,128)} async-done(((f32[16,1792]{1,0:T(8,128)}), f32[512,1792]{1,0:T(8,128)}) %all-gather.5.cloned.1.call-update) | async-done | bytes 3670032 | tf_op jit(solution)/shard_map/all_gather | solution.py:36
  423.0 125.6 %reduce-scatter.5.cloned.1.call-done = f32[16,1792]{1,0:T(8,128)} async-done(((f32[512,1792]{1,0:T(8,128)}), f32[16,1792]{1,0:T(8,128)}) %reduce-scatter.5.cloned.1.call-update) | async-done | bytes 114704 | tf_op jit(solution)/shard_map/reduce_scatter | solution.py:29
  548.7 0.0 copy-start.1
  548.7 3.8 fusion
  552.5 0.0 copy-start.2
  552.5 0.0 all-to-all-done
  552.5 0.0 copy-done.1
  552.6 4.6 add_divide_fusion
  557.1 84.7 %reduce-scatter.3.cloned.1.call-done = f32[256,512]{1,0:T(8,128)} async-done(((f32[256,4096]{1,0:T(8,128)}), f32[256,512]{1,0:T(8,128)}) %reduce-scatter.3.cloned.1.call-update) | async-done | bytes 524304 | tf_op jit(solution)/shard_map/reduce_scatter | solution.py:26
  641.8 0.0 copy-done.2
Async XLA Ops:
  7.2 3.9 copy-start
  7.2 94.8 %all-gather.3.cloned.1.call-start = ((), (), s32[]{:S(2)}) async-start(), calls=%async_computation.3 | async-start | bytes 15138816 | tf_op jit(solution)/shard_map/all_gather | solution.py:22
  7.9 346.5 %all-reduce.2.cloned.1.call-start = ((), (), s32[]{:S(2)}) async-start(), calls=%async_computation.5 | async-start | bytes 2097152 | tf_op jit(solution)/shard_map/psum | solution.py:28
  10.2 412.8 %all-gather.5.cloned.1.call-start = ((), (), s32[]{:S(2)}) async-start(), calls=%async_computation.7 | async-start | bytes 3784704 | tf_op jit(solution)/shard_map/all_gather | solution.py:36
  11.0 537.7 %reduce-scatter.5.cloned.1.call-start = ((), (), s32[]{:S(2)}) async-start(), calls=%async_computation.6 | async-start | bytes 3784704 | tf_op jit(solution)/shard_map/reduce_scatter | solution.py:29
  14.6 627.2 %reduce-scatter.3.cloned.1.call-start = ((), (), s32[]{:S(2)}) async-start(), calls=%async_computation.4 | async-start | bytes 4718592 | tf_op jit(solution)/shard_map/reduce_scatter | solution.py:26
  118.0 0.9 copy-start.3
  121.1 431.4 %all-to-all-start = ((f32[32,16,1792]{2,1,0:T(8,128)}), f32[32,16,1792]{2,1,0:T(8,128)}, u32[]{:S(2)}, u32[]{:S(2)}) async-start(f32[32,16,1792]{2,1,0:T(8,128)} %stack.2), calls=%async_computation.1 | async-start | bytes 7340032 | tf_op jit(solution)/shard_map/all_to_all | solution.py:34
  548.7 3.9 copy-start.1
  552.5 89.3 %copy-start.2 = (f32[16,1792]{1,0:T(8,128)}, f32[16,1792]{1,0:T(8,128)S(1)}, u32[]{:S(2)}) copy-start(f32[16,1792]{1,0:T(8,128)S(1)} %fusion) | copy-start | bytes 344068
Sparse Core Ops, SparseCore 0:
  9.8 92.0 all-gather.2
  104.6 249.7 all-reduce.1
  356.3 66.7 all-gather.4
  425.4 123.1 reduce-scatter.4
  553.3 88.4 reduce-scatter.2
